TPU v7x, 32 devices: a whole 2x2x4 slice. The times are simulated.
32 devices in a mesh: section: 8 (over z, core), tensor: 2 (over x), replica: 2 (over y).
Axes of the slice: x: 2, y: 2, z: 4, core: 2. Of those that a mesh axis runs over, the one named last changes fastest.
Arguments:
- pool_inputs: bfloat16 [8, 256, 2, 1408], P('section', 'replica', None, 'tensor'), may hold values from -6 to 6
- pool_mixed: bfloat16 [8, 256, 1408], P('section', 'replica'), may hold values from -6 to 6
- crop_ids: int32 [8, 8, 128], P('section', 'replica'), may hold values from 0 to 127
- incoming: bfloat16 [8, 256, 1408], P('section', 'replica', 'tensor'), may hold values from -6 to 6
- loss_grads: bfloat16 [3, 256, 1408], P(None, 'replica', 'tensor'), may hold values from -6 to 6
- w_proj: bfloat16 [8, 2, 1408, 1408], P('section', None, ('tensor', 'replica')), may hold values from -0.109375 to 0.109375
- w_up: bfloat16 [8, 1408, 3072], P('section', None, ('tensor', 'replica')), may hold values from -0.15625 to 0.15625
- w_down: bfloat16 [8, 3072, 1408], P('section', ('tensor', 'replica')), may hold values from -0.109375 to 0.109375
Outputs:
- grad_proj: bfloat16 [8, 2, 1408, 1408], P('section', None, ('tensor', 'replica'))
- grad_up: bfloat16 [8, 1408, 3072], P('section', None, ('tensor', 'replica'))
- grad_down: bfloat16 [8, 3072, 1408], P('section', ('tensor', 'replica'))
- outgoing: bfloat16 [8, 256, 2, 1408], P('section', 'replica', None, 'tensor')
All inputs are finite; a program needn't handle non-finite values.
Results may differ from a plain program's by a relative error of at most 0.02.
Values may be sent and summed in bfloat16 or wider, within the bound.
A program may use at most 128 MiB of HBM per device.

v0:
```python
import jax
import jax.numpy as jnp
from jax import lax
from jax.sharding import PartitionSpec as P

gelu_scale = 0.7978845608
gelu_cubic = 0.044715


def from_partner(value, axis, bit):
    mask = 2**bit
    pairs = [(source, source ^ mask) for source in range(lax.axis_size(axis))]
    return lax.ppermute(value, axis, pairs)


def shifted(x, axis, by):
    devices = lax.axis_size(axis)
    pairs = [(i, i + by) for i in range(devices) if 0 <= i + by < devices]
    return lax.ppermute(x, axis, pairs)


def gelu_pair(pre_gelu):
    inner = gelu_scale * (pre_gelu + gelu_cubic * pre_gelu * pre_gelu * pre_gelu)
    tanh_part = jnp.tanh(inner)
    gelu_value = 0.5 * pre_gelu * (1.0 + tanh_part)
    gelu_slope = 0.5 * (1.0 + tanh_part) + 0.5 * pre_gelu * (
        1.0 - tanh_part * tanh_part
    ) * gelu_scale * (1.0 + 3.0 * gelu_cubic * pre_gelu * pre_gelu)
    return (gelu_value, gelu_slope)


def reflect(block, section_count):
    for bit_number in range(section_count.bit_length() - 1):
        block = from_partner(block, "section", bit_number)
    return block


def body(pool_inputs, pool_mixed, crop_ids, incoming, loss_grads, w_proj, w_up, w_down):
    section_index = lax.axis_index("section")
    section_count = lax.axis_size("section")
    proj_full, up_full, down_full = (
        lax.all_gather(w_proj, "replica", axis=2, tiled=True),
        lax.all_gather(w_up, "replica", axis=2, tiled=True),
        lax.all_gather(w_down, "replica", axis=1, tiled=True),
    )
    proj_local = proj_full[0]
    up_local = up_full[0]
    down_local = down_full[0]
    seed_full, loss_full = (
        lax.all_gather(incoming, "tensor", axis=2, tiled=True),
        lax.all_gather(loss_grads, "tensor", axis=2, tiled=True),
    )
    encoder = section_index < section_count // 2
    decoder_flag = jnp.where(encoder, 0.0, 1.0).astype(jnp.bfloat16)
    skip_mask = jnp.stack([jnp.ones((), jnp.bfloat16), decoder_flag])[None, :, None]
    encoder_weight = jnp.where(encoder, 1.0, 0.0).astype(jnp.float32)
    is_top = section_index == section_count - 1
    tick_count = crop_ids.shape[1]
    upstream = seed_full[0]
    kept_inputs, kept_mixed, kept_active, kept_hidden, kept_grads, kept_upstream = (
        [],
        [],
        [],
        [],
        [],
        [],
    )
    input_grad = None
    for tick_index in range(tick_count):
        picked_rows = crop_ids[0, tick_index]
        inputs = pool_inputs[0][picked_rows] * skip_mask
        mixed_rows = pool_mixed[0][picked_rows]
        pre_gelu = jnp.dot(mixed_rows, up_local, preferred_element_type=jnp.float32)
        gelu_value, gelu_slope = gelu_pair(pre_gelu)
        activated = gelu_value.astype(jnp.bfloat16)
        back_act = jnp.einsum("md,fd->mf", upstream, down_local, preferred_element_type=jnp.float32)
        back_hidden = (back_act * gelu_slope).astype(jnp.bfloat16)
        partial_back = jnp.einsum(
            "mf,df->md", back_hidden, up_local, preferred_element_type=jnp.float32
        )
        back_mixed = upstream.astype(jnp.float32) + lax.psum(partial_back, "tensor")
        mixed_grad = back_mixed.astype(jnp.bfloat16)
        input_grad = jnp.einsum(
            "mj,kij->mki", mixed_grad, proj_local, preferred_element_type=jnp.float32
        ).astype(jnp.bfloat16)
        kept_inputs.append(inputs)
        kept_mixed.append(mixed_rows)
        kept_active.append(activated)
        kept_hidden.append(back_hidden)
        kept_grads.append(mixed_grad)
        kept_upstream.append(upstream)
        if tick_index + 1 < tick_count:
            from_above = shifted(input_grad[:, 0], "section", -1)
            mirrored = reflect(input_grad[:, 1], section_count)
            summed = (
                from_above.astype(jnp.float32) + encoder_weight * mirrored.astype(jnp.float32)
            ).astype(jnp.bfloat16)
            summed = lax.all_gather(summed, "tensor", axis=1, tiled=True)
            upstream = jnp.where(is_top, loss_full[tick_index], summed)
    all_inputs = jnp.concatenate(kept_inputs, axis=0)
    all_mixed = jnp.concatenate(kept_mixed, axis=0)
    all_active = jnp.concatenate(kept_active, axis=0)
    all_hidden = jnp.concatenate(kept_hidden, axis=0)
    all_grads = jnp.concatenate(kept_grads, axis=0)
    all_upstream = jnp.concatenate(kept_upstream, axis=0)
    down_total = jnp.einsum(
        "mf,md->fd", all_active, all_upstream, preferred_element_type=jnp.float32
    )
    up_total = jnp.einsum("md,mf->df", all_mixed, all_hidden, preferred_element_type=jnp.float32)
    proj_total = jnp.einsum(
        "mki,mj->kij", all_inputs, all_grads, preferred_element_type=jnp.float32
    )
    reduced = (
        lax.psum_scatter(
            proj_total[None].astype(jnp.bfloat16), "replica", scatter_dimension=2, tiled=True
        ).astype(jnp.float32),
        lax.psum_scatter(
            up_total[None].astype(jnp.bfloat16), "replica", scatter_dimension=2, tiled=True
        ).astype(jnp.float32),
        lax.psum_scatter(
            down_total[None].astype(jnp.bfloat16), "replica", scatter_dimension=1, tiled=True
        ).astype(jnp.float32),
    )
    return (
        reduced[0].astype(jnp.bfloat16),
        reduced[1].astype(jnp.bfloat16),
        reduced[2].astype(jnp.bfloat16),
        input_grad[None],
    )


def solution(mesh):
    in_specs = (
        P("section", "replica", None, "tensor"),
        P("section", "replica", None),
        P("section", "replica", None),
        P("section", "replica", "tensor"),
        P(None, "replica", "tensor"),
        P("section", None, ("tensor", "replica"), None),
        P("section", None, ("tensor", "replica")),
        P("section", ("tensor", "replica"), None),
    )
    out_specs = (
        P("section", None, ("tensor", "replica"), None),
        P("section", None, ("tensor", "replica")),
        P("section", ("tensor", "replica"), None),
        P("section", "replica", None, "tensor"),
    )
    return jax.shard_map(body, mesh=mesh, in_specs=in_specs, out_specs=out_specs, check_vma=False)
```

profile of v0, /device:TPU:0, one launch (start us, length us, event | category | flops | bytes accessed | tf_op | source)
XLA Modules:
  0.0 637.9 jit_solution(14734872152342492354)
XLA Ops:
  9.7 8.2 %all_gather.24 = bf16[1,128,1408]{1,2,0:T(8,128)(2,1)S(1)} all-gather(bf16[1,128,704]{1,2,0:T(8,128)(2,1)S(1)} %copy-done.23), channel_id=1, replica_groups=mesh['section'=8,'tensor'=2,'replica'=2] {'tensor'}, dimensions={2}, use_global_device_ids=true | all-gather | bytes 540672 | tf_op jit(solution)/shard_map/all_gather | solution.py:50
  17.9 52.6 %all-gather.7.cloned.1.call-done = bf16[1,1408,1536]{2,1,0:T(8,128)(2,1)} async-done(((bf16[1,1408,768]{2,1,0:T(8,128)(2,1)}), bf16[1,1408,1536]{2,1,0:T(8,128)(2,1)}) %all-gather.7.cloned.1.call-update) | async-done | bytes 4325392 | tf_op jit(solution)/shard_map/all_gather | solution.py:43
  70.5 4.0 multiply_convert_fusion.3
  74.5 55.8 %all-gather.5.cloned.1.call-done = bf16[1,1536,1408]{2,1,0:T(8,128)(2,1)} async-done(((bf16[1,768,1408]{2,1,0:T(8,128)(2,1)}), bf16[1,1536,1408]{2,1,0:T(8,128)(2,1)}) %all-gather.5.cloned.1.call-update) | async-done | bytes 4325392 | tf_op jit(solution)/shard_map/all_gather | solution.py:44
  130.3 4.0 fusion.56
  138.9 31.7 %all-reduce.5.cloned.1.call-done = f32[128,1408]{1,0:T(8,128)} async-done(((f32[128,1408]{1,0:T(8,128)}), f32[128,1408]{1,0:T(8,128)}) %all-reduce.5.cloned.1.call-update) | async-done | bytes 720912 | tf_op jit(solution)/shard_map/psum | solution.py:81
  171.7 54.4 %all-gather.11.cloned.1.call-done = bf16[1,2,704,1408]{3,2,1,0:T(8,128)(2,1)} async-done(((bf16[1,2,352,1408]{3,2,1,0:T(8,128)(2,1)}), bf16[1,2,704,1408]{3,2,1,0:T(8,128)(2,1)}) %all-gather.11.cloned.1.call-update) | async-done | bytes 3964944 | tf_op jit(solution)/shard_map/all_gather | solution.py:42
  232.4 16.7 %all-gather.9.cloned.1.call-done = bf16[3,128,1408]{1,2,0:T(8,128)(2,1)} async-done(((bf16[3,128,704]{1,2,0:T(8,128)(2,1)}), bf16[3,128,1408]{1,2,0:T(8,128)(2,1)}) %all-gather.9.cloned.1.call-update) | async-done | bytes 1081360 | tf_op jit(solution)/shard_map/all_gather | solution.py:51
  255.1 4.2 multiply_convert_fusion.2
  259.2 6.9 %collective-permute-done.3 = bf16[128,704]{0,1:T(8,128)(2,1)S(1)} collective-permute-done((bf16[128,704]{0,1:T(8,128)(2,1)S(1)}, bf16[128,704]{0,1:T(8,128)(2,1)S(1)}, u32[]{:S(2)}, u32[]{:S(2)}) %collective-permute-start.3) | collective-permute-done | bytes 180256 | tf_op jit(solution)/shard_map/ppermute | solution.py:13
  266.2 6.2 all_gather.29
  272.7 4.2 fusion.53
  280.1 32.3 %all-reduce.7.cloned.1.call-done = f32[128,1408]{1,0:T(8,128)} async-done(((f32[128,1408]{1,0:T(8,128)}), f32[128,1408]{1,0:T(8,128)}) %all-reduce.7.cloned.1.call-update) | async-done | bytes 720912 | tf_op jit(solution)/shard_map/psum | solution.py:81
  313.6 3.5 fusion.103
  327.6 4.1 multiply_convert_fusion.1
  331.7 5.0 collective-permute-done.7
  336.7 6.4 %all_gather.30 = bf16[128,1408]{0,1:T(8,128)(2,1)S(1)} all-gather(bf16[128,704]{0,1:T(8,128)(2,1)S(1)} %add_convert_fusion.5), channel_id=1, replica_groups=mesh['section'=8,'tensor'=2,'replica'=2] {'tensor'}, dimensions={1}, use_global_device_ids=true | all-gather | bytes 540672 | tf_op jit(solution)/shard_map/all_gather | solution.py:98
  343.4 4.2 fusion.50
  350.9 32.9 %all-reduce.9.cloned.1.call-done = f32[128,1408]{1,0:T(8,128)} async-done(((f32[128,1408]{1,0:T(8,128)}), f32[128,1408]{1,0:T(8,128)}) %all-reduce.9.cloned.1.call-update) | async-done | bytes 720912 | tf_op jit(solution)/shard_map/psum | solution.py:81
  385.0 3.4 fusion.106
  399.0 4.1 multiply_convert_fusion
  403.1 5.0 collective-permute-done.11
  408.2 6.2 all_gather.31
  414.6 4.2 fusion.47
  432.3 22.7 %all-reduce.11.cloned.1.call-done = f32[128,1408]{1,0:T(8,128)} async-done(((f32[128,1408]{1,0:T(8,128)}), f32[128,1408]{1,0:T(8,128)}) %all-reduce.11.cloned.1.call-update) | async-done | bytes 720912 | tf_op jit(solution)/shard_map/psum | solution.py:81
  456.3 5.7 fusion.34
  463.6 5.6 fusion
  470.8 4.6 fusion.1
  475.4 4.2 fusion.112
  479.6 34.5 %reduce-scatter.4.cloned.1.call-done = bf16[1,2,352,1408]{3,2,1,0:T(8,128)(2,1)} async-done(((bf16[1,2,704,1408]{3,2,1,0:T(8,128)(2,1)}), bf16[1,2,352,1408]{3,2,1,0:T(8,128)(2,1)}) %reduce-scatter.4.cloned.1.call-update) | async-done | bytes 1982480 | tf_op jit(solution)/shard_map/reduce_scatter | solution.py:114
  514.1 58.5 %reduce-scatter.6.cloned.1.call-done = bf16[1,1408,768]{2,1,0:T(8,128)(2,1)} async-done(((bf16[1,1408,1536]{2,1,0:T(8,128)(2,1)}), bf16[1,1408,768]{2,1,0:T(8,128)(2,1)}) %reduce-scatter.6.cloned.1.call-update) | async-done | bytes 2162704 | tf_op jit(solution)/shard_map/reduce_scatter | solution.py:117
  572.7 58.7 %reduce-scatter.8.cloned.1.call-done = bf16[1,768,1408]{2,1,0:T(8,128)(2,1)} async-done(((bf16[1,1536,1408]{2,1,0:T(8,128)(2,1)}), bf16[1,768,1408]{2,1,0:T(8,128)(2,1)}) %reduce-scatter.8.cloned.1.call-update) | async-done | bytes 2162704 | tf_op jit(solution)/shard_map/reduce_scatter | solution.py:120
  (167 shorter events, 68.6 us)
Async XLA Ops:
  7.2 63.3 %all-gather.7.cloned.1.call-start = ((), (), s32[]{:S(2)}) async-start(), calls=%async_computation.4 | async-start | bytes 6488064 | tf_op jit(solution)/shard_map/all_gather | solution.py:43
  7.9 122.3 %all-gather.5.cloned.1.call-start = ((), (), s32[]{:S(2)}) async-start(), calls=%async_computation.3 | async-start | bytes 6488064 | tf_op jit(solution)/shard_map/all_gather | solution.py:44
  8.7 161.8 %all-reduce.5.cloned.1.call-start = ((), (), s32[]{:S(2)}) async-start(), calls=%async_computation.5 | async-start | bytes 1441792 | tf_op jit(solution)/shard_map/psum | solution.py:81
  9.7 64.8 %copy-start.17 = (bf16[128,1408]{1,0:T(8,128)(2,1)}, bf16[128,1408]{1,0:T(8,128)(2,1)S(1)}, u32[]{:S(2)}) copy-start(bf16[128,1408]{1,0:T(8,128)(2,1)S(1)} %gather_fusion.4) | copy-start | bytes 1081348
  70.5 64.5 %slice-start = ((s8[4325376]{0:T(1024)(128)(4,1)}), s8[131072]{0:T(1024)(128)(4,1)S(1)}, s32[]{:S(2)}) async-start(s8[4325376]{0:T(1024)(128)(4,1)} %bitcast.149), calls=%async_computation.14 | async-start | bytes 262144
  137.4 88.7 %all-gather.11.cloned.1.call-start = ((), (), s32[]{:S(2)}) async-start(), calls=%async_computation.7 | async-start | bytes 5947392 | tf_op jit(solution)/shard_map/all_gather | solution.py:42
  138.0 111.2 %all-gather.9.cloned.1.call-start = ((), (), s32[]{:S(2)}) async-start(), calls=%async_computation.6 | async-start | bytes 1622016 | tf_op jit(solution)/shard_map/all_gather | solution.py:51
  138.6 173.8 %all-reduce.7.cloned.1.call-start = ((), (), s32[]{:S(2)}) async-start(), calls=%async_computation.8 | async-start | bytes 1441792 | tf_op jit(solution)/shard_map/psum | solution.py:81
  229.5 1.5 collective-permute-start.1
  230.5 28.8 %copy-start.19 = (bf16[128,1408]{1,0:T(8,128)(2,1)}, bf16[128,1408]{1,0:T(8,128)(2,1)S(1)}, u32[]{:S(2)}) copy-start(bf16[128,1408]{1,0:T(8,128)(2,1)S(1)} %gather_fusion.5) | copy-start | bytes 1081348
  230.9 21.0 %collective-permute-start.2 = (bf16[128,704]{0,1:T(8,128)(2,1)S(1)}, bf16[128,704]{0,1:T(8,128)(2,1)S(1)}, u32[]{:S(2)}, u32[]{:S(2)}) collective-permute-start(bf16[128,704]{0,1:T(8,128)(2,1)S(1)} %collective-permute-done.1), channel_id=1, source_target_pairs={{0,8},{4,12},{8,0},{12,4},{16,24},{20,28},{24,16},{28,20},{1,9},{5... | collective-permute-start | bytes 540680 | tf_op jit(solution)/shard_map/ppermute | solution.py:13
  250.7 8.6 %collective-permute-start = (bf16[128,704]{0,1:T(8,128)(2,1)S(1)}, bf16[128,704]{0,1:T(8,128)(2,1)S(1)}, u32[]{:S(2)}, u32[]{:S(2)}) collective-permute-start(bf16[128,704]{0,1:T(8,128)(2,1)S(1)} %get-tuple-element.11), channel_id=1, source_target_pairs={{4,0},{8,4},{12,8},{16,12},{20,16},{24,20},{28,24},{5,1},{9,5},{13... | collective-permute-start | bytes 540680 | tf_op jit(solution)/shard_map/ppermute | solution.py:19
  252.0 14.2 %collective-permute-start.3 = (bf16[128,704]{0,1:T(8,128)(2,1)S(1)}, bf16[128,704]{0,1:T(8,128)(2,1)S(1)}, u32[]{:S(2)}, u32[]{:S(2)}) collective-permute-start(bf16[128,704]{0,1:T(8,128)(2,1)S(1)} %collective-permute-done.2), channel_id=1, source_target_pairs={{0,16},{4,20},{8,24},{12,28},{16,0},{20,4},{24,8},{28,12},{1,17},{... | collective-permute-start | bytes 540680 | tf_op jit(solution)/shard_map/ppermute | solution.py:13
  280.0 103.7 %all-reduce.9.cloned.1.call-start = ((), (), s32[]{:S(2)}) async-start(), calls=%async_computation.9 | async-start | bytes 1441792 | tf_op jit(solution)/shard_map/psum | solution.py:81
  317.1 1.5 collective-permute-start.5
  318.6 6.6 %collective-permute-start.6 = (bf16[128,704]{0,1:T(8,128)(2,1)S(1)}, bf16[128,704]{0,1:T(8,128)(2,1)S(1)}, u32[]{:S(2)}, u32[]{:S(2)}) collective-permute-start(bf16[128,704]{0,1:T(8,128)(2,1)S(1)} %collective-permute-done.5), channel_id=1, source_target_pairs={{0,8},{4,12},{8,0},{12,4},{16,24},{20,28},{24,16},{28,20},{1,9},{5... | collective-permute-start | bytes 540680 | tf_op jit(solution)/shard_map/ppermute | solution.py:13
  320.9 10.7 %copy-start.21 = (bf16[128,1408]{1,0:T(8,128)(2,1)}, bf16[128,1408]{1,0:T(8,128)(2,1)S(1)}, u32[]{:S(2)}) copy-start(bf16[128,1408]{1,0:T(8,128)(2,1)S(1)} %gather_fusion.6) | copy-start | bytes 1081348
  321.2 10.5 %collective-permute-start.4 = (bf16[128,704]{0,1:T(8,128)(2,1)S(1)}, bf16[128,704]{0,1:T(8,128)(2,1)S(1)}, u32[]{:S(2)}, u32[]{:S(2)}) collective-permute-start(bf16[128,704]{0,1:T(8,128)(2,1)S(1)} %get-tuple-element.9), channel_id=1, source_target_pairs={{4,0},{8,4},{12,8},{16,12},{20,16},{24,20},{28,24},{5,1},{9,5},{13... | collective-permute-start | bytes 540680 | tf_op jit(solution)/shard_map/ppermute | solution.py:19
  325.1 11.5 %collective-permute-start.7 = (bf16[128,704]{0,1:T(8,128)(2,1)S(1)}, bf16[128,704]{0,1:T(8,128)(2,1)S(1)}, u32[]{:S(2)}, u32[]{:S(2)}) collective-permute-start(bf16[128,704]{0,1:T(8,128)(2,1)S(1)} %collective-permute-done.6), channel_id=1, source_target_pairs={{0,16},{4,20},{8,24},{12,28},{16,0},{20,4},{24,8},{28,12},{1,17},{... | collective-permute-start | bytes 540680 | tf_op jit(solution)/shard_map/ppermute | solution.py:13
  343.3 5.1 slice-start.4
  343.4 40.4 %copy-start.3 = (bf16[128,1408]{1,0:T(8,128)(2,1)}, bf16[128,1408]{1,0:T(8,128)(2,1)S(1)}, u32[]{:S(2)}) copy-start(bf16[128,1408]{1,0:T(8,128)(2,1)S(1)} %bitcast_select_fusion.1) | copy-start | bytes 1081348
  350.8 104.2 %all-reduce.11.cloned.1.call-start = ((), (), s32[]{:S(2)}) async-start(), calls=%async_computation.10 | async-start | bytes 1441792 | tf_op jit(solution)/shard_map/psum | solution.py:81
  388.5 1.5 collective-permute-start.9
  389.9 6.6 %collective-permute-start.10 = (bf16[128,704]{0,1:T(8,128)(2,1)S(1)}, bf16[128,704]{0,1:T(8,128)(2,1)S(1)}, u32[]{:S(2)}, u32[]{:S(2)}) collective-permute-start(bf16[128,704]{0,1:T(8,128)(2,1)S(1)} %collective-permute-done.9), channel_id=1, source_target_pairs={{0,8},{4,12},{8,0},{12,4},{16,24},{20,28},{24,16},{28,20},{1,9},{5... | collective-permute-start | bytes 540680 | tf_op jit(solution)/shard_map/ppermute | solution.py:13
  392.3 10.7 %copy-start.22 = (bf16[128,1408]{1,0:T(8,128)(2,1)}, bf16[128,1408]{1,0:T(8,128)(2,1)S(1)}, u32[]{:S(2)}) copy-start(bf16[128,1408]{1,0:T(8,128)(2,1)S(1)} %gather_fusion.7) | copy-start | bytes 1081348
  392.6 10.5 %collective-permute-start.8 = (bf16[128,704]{0,1:T(8,128)(2,1)S(1)}, bf16[128,704]{0,1:T(8,128)(2,1)S(1)}, u32[]{:S(2)}, u32[]{:S(2)}) collective-permute-start(bf16[128,704]{0,1:T(8,128)(2,1)S(1)} %get-tuple-element.7), channel_id=1, source_target_pairs={{4,0},{8,4},{12,8},{16,12},{20,16},{24,20},{28,24},{5,1},{9,5},{13... | collective-permute-start | bytes 540680 | tf_op jit(solution)/shard_map/ppermute | solution.py:19
  396.5 11.5 %collective-permute-start.11 = (bf16[128,704]{0,1:T(8,128)(2,1)S(1)}, bf16[128,704]{0,1:T(8,128)(2,1)S(1)}, u32[]{:S(2)}, u32[]{:S(2)}) collective-permute-start(bf16[128,704]{0,1:T(8,128)(2,1)S(1)} %collective-permute-done.10), channel_id=1, source_target_pairs={{0,16},{4,20},{8,24},{12,28},{16,0},{20,4},{24,8},{28,12},{1,17},{... | collective-permute-start | bytes 540680 | tf_op jit(solution)/shard_map/ppermute | solution.py:13
  414.3 5.3 slice-start.6
  422.0 92.1 %reduce-scatter.4.cloned.1.call-start = ((), (), s32[]{:S(2)}) async-start(), calls=%async_computation.11 | async-start | bytes 5947392 | tf_op jit(solution)/shard_map/reduce_scatter | solution.py:114
  462.0 110.6 %reduce-scatter.6.cloned.1.call-start = ((), (), s32[]{:S(2)}) async-start(), calls=%async_computation.12 | async-start | bytes 6488064 | tf_op jit(solution)/shard_map/reduce_scatter | solution.py:117
  469.2 162.2 %reduce-scatter.8.cloned.1.call-start = ((), (), s32[]{:S(2)}) async-start(), calls=%async_computation.13 | async-start | bytes 6488064 | tf_op jit(solution)/shard_map/reduce_scatter | solution.py:120
  475.4 156.0 %copy-start.1 = (bf16[1,128,1408]{2,1,0:T(8,128)(2,1)S(1)}, bf16[1,128,1408]{2,1,0:T(8,128)(2,1)}, u32[]{:S(2)}) copy-start(bf16[1,128,1408]{2,1,0:T(8,128)(2,1)} %param.9) | copy-start | bytes 1081348
  (28 other events, 62.0 us)
Sparse Core Ops, SparseCore 0:
  9.5 60.9 all-gather.6
  72.0 58.1 all-gather.4
  137.6 32.9 all-reduce.4
  171.9 54.1 all-gather.10
  227.5 21.6 all-gather.8
  280.2 32.1 all-reduce.6
  350.9 32.8 all-reduce.8
  422.1 32.8 all-reduce.10
  462.2 51.8 reduce-scatter.3
  516.8 55.7 reduce-scatter.5
  575.6 55.7 reduce-scatter.7
where the time goes:
time: 639 us; the launch traced here: 638 us
  waiting for transfers between devices  479 us (75%)
  matrix products  72.9 us (11%)
  blocking collectives  26.9 us (4%)
  local copies, waits for them, and re-layouts  21 us (3%)
  starting transfers between devices  17.4 us (3%)
  between operations  14.5 us (2%)
    psum x4, waiting for transfers between devices, body(): back_mixed = upstream.astype(jnp.float32) + lax.psum(partial_back, 'tensor')  120 us
    reduce_scatter x1, waiting for transfers between devices, body(): lax.psum_scatter(down_total[None].astype(jnp.bfloat16), 'replica', scatte...  58.7 us
    reduce_scatter x1, waiting for transfers between devices, body(): lax.psum_scatter(up_total[None].astype(jnp.bfloat16), 'replica', scatter_...  58.5 us
    all_gather x1, waiting for transfers between devices, body(): lax.all_gather(w_down, 'replica', axis=1, tiled=True)  55.8 us
    all_gather x1, waiting for transfers between devices, body(): lax.all_gather(w_proj, 'replica', axis=2, tiled=True)  54.4 us
    all_gather x1, waiting for transfers between devices, body(): lax.all_gather(w_up, 'replica', axis=2, tiled=True)  52.6 us
    reduce_scatter x1, waiting for transfers between devices, body(): lax.psum_scatter(proj_total[None].astype(jnp.bfloat16), 'replica', scatte...  34.5 us
    ppermute x9, waiting for transfers between devices, from_partner(): return lax.ppermute(value, axis, pairs)  25.6 us
  transfers between devices with their start and end apart: 23, of which 19 were waited for; matrix products, arithmetic and copies ran while one was open for 8% of the time, Pallas kernels for 0%

commit v1 on v0

--- a/solution.py
+++ b/solution.py
@@ -1,3 +1,4 @@
+import functools
 import jax
 import jax.numpy as jnp
 from jax import lax
@@ -5,6 +6,14 @@
 
 gelu_scale = 0.7978845608
 gelu_cubic = 0.044715
+
+
+def _keep_up_rounds(row_data, comm_axis):
+    current_arr = lax.ppermute(row_data, comm_axis, [(0, 1), (1, 0)])
+    return row_data + current_arr
+
+
+post_teams = functools.partial(_keep_up_rounds, comm_axis="tensor")
 
 
 def from_partner(value, axis, bit):
@@ -78,7 +87,7 @@
         partial_back = jnp.einsum(
             "mf,df->md", back_hidden, up_local, preferred_element_type=jnp.float32
         )
-        back_mixed = upstream.astype(jnp.float32) + lax.psum(partial_back, "tensor")
+        back_mixed = upstream.astype(jnp.float32) + post_teams(partial_back)
         mixed_grad = back_mixed.astype(jnp.bfloat16)
         input_grad = jnp.einsum(
             "mj,kij->mki", mixed_grad, proj_local, preferred_element_type=jnp.float32

time: 639 us -> 538 us (0.84)
  waiting for transfers between devices: 479 us -> 389 us
  matrix products: 72.9 us -> 63 us
    psum x4 -> x0, waiting for transfers between devices: 120 us -> none  [body(): back_mixed = upstream.astype(jnp.float32) + lax.psum(partial_back, 'tensor')]
    ppermute x0 -> x4, waiting for transfers between devices: none -> 52 us  [_keep_up_rounds(): current_arr = lax.ppermute(row_data, comm_axis, [(0, 1), (1, 0)])]
    all_gather x1, waiting for transfers between devices: 54.4 us -> 32.3 us  [body(): lax.all_gather(w_proj, 'replica', axis=2, tiled=True)]
  transfers between devices with their start and end apart: 23 -> 23, of which waited for: 19 -> 19; matrix products, arithmetic and copies ran while one was open for 8% -> 10% of each run, Pallas kernels for 0% -> 0%
where the time goes in v1:
time: 538 us
  waiting for transfers between devices  389 us (72%)
  matrix products  63 us (12%)
  blocking collectives  26.8 us (5%)
  starting transfers between devices  22.9 us (4%)
  local copies, waits for them, and re-layouts  18.6 us (3%)
  between operations  14.9 us (3%)
    reduce_scatter x1, waiting for transfers between devices, body(): lax.psum_scatter(down_total[None].astype(jnp.bfloat16), 'replica', scatte...  58.7 us
    reduce_scatter x1, waiting for transfers between devices, body(): lax.psum_scatter(up_total[None].astype(jnp.bfloat16), 'replica', scatter_...  58.6 us
    all_gather x1, waiting for transfers between devices, body(): lax.all_gather(w_down, 'replica', axis=1, tiled=True)  55.8 us
    ppermute x4, waiting for transfers between devices, _keep_up_rounds(): current_arr = lax.ppermute(row_data, comm_axis, [(0, 1), (1, 0)])  52 us
    all_gather x1, waiting for transfers between devices, body(): lax.all_gather(w_up, 'replica', axis=2, tiled=True)  51.9 us
    reduce_scatter x1, waiting for transfers between devices, body(): lax.psum_scatter(proj_total[None].astype(jnp.bfloat16), 'replica', scatte...  35.5 us
    all_gather x1, waiting for transfers between devices, body(): lax.all_gather(w_proj, 'replica', axis=2, tiled=True)  32.3 us
    ppermute x9, waiting for transfers between devices, from_partner(): return lax.ppermute(value, axis, pairs)  25.7 us
  transfers between devices with their start and end apart: 23, of which 19 were waited for; matrix products, arithmetic and copies ran while one was open for 10% of the time, Pallas kernels for 0%

profile of v1, /device:TPU:0, one launch (start us, length us, event | category | flops | bytes accessed | tf_op | source)
XLA Modules:
  0.0 538.0 jit_solution(15578161076167166799)
XLA Ops:
  10.4 8.2 %all_gather.24 = bf16[1,128,1408]{1,2,0:T(8,128)(2,1)S(1)} all-gather(bf16[1,128,704]{1,2,0:T(8,128)(2,1)S(1)} %copy-done.31), channel_id=1, replica_groups=mesh['section'=8,'tensor'=2,'replica'=2] {'tensor'}, dimensions={2}, use_global_device_ids=true | all-gather | bytes 540672 | tf_op jit(solution)/shard_map/all_gather | solution.py:59
  18.6 51.9 %all-gather.7.cloned.1.call-done = bf16[1,1408,1536]{2,1,0:T(8,128)(2,1)} async-done(((bf16[1,1408,768]{2,1,0:T(8,128)(2,1)}), bf16[1,1408,1536]{2,1,0:T(8,128)(2,1)}) %all-gather.7.cloned.1.call-update) | async-done | bytes 4325392 | tf_op jit(solution)/shard_map/all_gather | solution.py:52
  70.5 4.0 multiply_convert_fusion.3
  74.5 55.8 %all-gather.5.cloned.1.call-done = bf16[1,1536,1408]{2,1,0:T(8,128)(2,1)} async-done(((bf16[1,768,1408]{2,1,0:T(8,128)(2,1)}), bf16[1,1536,1408]{2,1,0:T(8,128)(2,1)}) %all-gather.5.cloned.1.call-update) | async-done | bytes 4325392 | tf_op jit(solution)/shard_map/all_gather | solution.py:53
  130.3 4.0 fusion.56
  137.7 16.0 %collective-permute-done = f32[128,1408]{1,0:T(8,128)S(1)} collective-permute-done((f32[128,1408]{1,0:T(8,128)S(1)}, f32[128,1408]{1,0:T(8,128)S(1)}, u32[]{:S(2)}, u32[]{:S(2)}) %collective-permute-start) | collective-permute-done | bytes 720928 | tf_op jit(solution)/shard_map/ppermute | solution.py:12
  153.7 32.3 %all-gather.11.cloned.1.call-done = bf16[1,2,704,1408]{3,2,1,0:T(8,128)(2,1)} async-done(((bf16[1,2,352,1408]{3,2,1,0:T(8,128)(2,1)}), bf16[1,2,704,1408]{3,2,1,0:T(8,128)(2,1)}) %all-gather.11.cloned.1.call-update) | async-done | bytes 3964944 | tf_op jit(solution)/shard_map/all_gather | solution.py:51
  192.3 16.8 %all-gather.9.cloned.1.call-done = bf16[3,128,1408]{1,2,0:T(8,128)(2,1)} async-done(((bf16[3,128,704]{1,2,0:T(8,128)(2,1)}), bf16[3,128,1408]{1,2,0:T(8,128)(2,1)}) %all-gather.9.cloned.1.call-update) | async-done | bytes 1081360 | tf_op jit(solution)/shard_map/all_gather | solution.py:60
  215.0 4.2 multiply_convert_fusion.2
  219.1 6.9 %collective-permute-done.4 = bf16[128,704]{0,1:T(8,128)(2,1)S(1)} collective-permute-done((bf16[128,704]{0,1:T(8,128)(2,1)S(1)}, bf16[128,704]{0,1:T(8,128)(2,1)S(1)}, u32[]{:S(2)}, u32[]{:S(2)}) %collective-permute-start.4) | collective-permute-done | bytes 180256 | tf_op jit(solution)/shard_map/ppermute | solution.py:22
  226.1 6.2 %all_gather.29 = bf16[128,1408]{0,1:T(8,128)(2,1)S(1)} all-gather(bf16[128,704]{0,1:T(8,128)(2,1)S(1)} %add_convert_fusion.6), channel_id=1, replica_groups=mesh['section'=8,'tensor'=2,'replica'=2] {'tensor'}, dimensions={1}, use_global_device_ids=true | all-gather | bytes 540672 | tf_op jit(solution)/shard_map/all_gather | solution.py:107
  232.6 4.2 fusion.53
  238.9 14.7 %collective-permute-done.5 = f32[128,1408]{1,0:T(8,128)S(1)} collective-permute-done((f32[128,1408]{1,0:T(8,128)S(1)}, f32[128,1408]{1,0:T(8,128)S(1)}, u32[]{:S(2)}, u32[]{:S(2)}) %collective-permute-start.5) | collective-permute-done | bytes 720928 | tf_op jit(solution)/shard_map/ppermute | solution.py:12
  263.1 3.4 collective-permute-start.9
  266.5 4.2 multiply_convert_fusion.1
  270.7 5.2 collective-permute-done.9
  276.0 6.3 %all_gather.30 = bf16[128,1408]{0,1:T(8,128)(2,1)S(1)} all-gather(bf16[128,704]{0,1:T(8,128)(2,1)S(1)} %add_convert_fusion.5), channel_id=1, replica_groups=mesh['section'=8,'tensor'=2,'replica'=2] {'tensor'}, dimensions={1}, use_global_device_ids=true | all-gather | bytes 540672 | tf_op jit(solution)/shard_map/all_gather | solution.py:107
  282.6 4.2 fusion.50
  289.0 15.2 %collective-permute-done.10 = f32[128,1408]{1,0:T(8,128)S(1)} collective-permute-done((f32[128,1408]{1,0:T(8,128)S(1)}, f32[128,1408]{1,0:T(8,128)S(1)}, u32[]{:S(2)}, u32[]{:S(2)}) %collective-permute-start.10) | collective-permute-done | bytes 720928 | tf_op jit(solution)/shard_map/ppermute | solution.py:12
  313.9 3.4 collective-permute-start.14
  317.2 3.9 multiply_convert_fusion
  321.2 5.5 %collective-permute-done.14 = bf16[128,704]{0,1:T(8,128)(2,1)S(1)} collective-permute-done((bf16[128,704]{0,1:T(8,128)(2,1)S(1)}, bf16[128,704]{0,1:T(8,128)(2,1)S(1)}, u32[]{:S(2)}, u32[]{:S(2)}) %collective-permute-start.14) | collective-permute-done | bytes 180256 | tf_op jit(solution)/shard_map/ppermute | solution.py:22
  326.7 6.2 %all_gather.31 = bf16[128,1408]{0,1:T(8,128)(2,1)S(1)} all-gather(bf16[128,704]{0,1:T(8,128)(2,1)S(1)} %add_convert_fusion.4), channel_id=1, replica_groups=mesh['section'=8,'tensor'=2,'replica'=2] {'tensor'}, dimensions={1}, use_global_device_ids=true | all-gather | bytes 540672 | tf_op jit(solution)/shard_map/all_gather | solution.py:107
  333.1 4.0 fusion.47
  348.5 6.2 %collective-permute-done.15 = f32[128,1408]{1,0:T(8,128)} collective-permute-done((f32[128,1408]{1,0:T(8,128)S(1)}, f32[128,1408]{1,0:T(8,128)}, u32[]{:S(2)}, u32[]{:S(2)}) %collective-permute-start.15) | collective-permute-done | bytes 720928 | tf_op jit(solution)/shard_map/ppermute | solution.py:12
  356.0 4.3 fusion.34
  361.9 5.5 %fusion = bf16[1,1408,1536]{2,1,0:T(8,128)(2,1)} fusion(bf16[128,1536]{1,0:T(8,128)(2,1)S(1)} %copy-done.23, bf16[128,1536]{1,0:T(8,128)(2,1)S(1)} %copy-done.21, bf16[128,1536]{1,0:T(8,128)(2,1)S(1)} %copy-done.19, bf16[128,1536]{1,0:T(8,128)(2,1)S(1)} %copy-done.17, bf16[128,1408]{1,0:T(8,128)(2,1)} %copy-done.30, bf16[128,1408]{1,0:T(8,128)(2,1)} %copy-done.29, ...), kind=kOutput, calls=%fused_computation.10 | convolution fusion | flops 2228813824 | bytes 7340032 | tf_op jit(solution)/shard_map/md,mf->df/dot_general | solution.py:118
  369.5 4.6 fusion.1
  374.1 4.1 fusion.112
  378.2 35.5 %reduce-scatter.4.cloned.1.call-done = bf16[1,2,352,1408]{3,2,1,0:T(8,128)(2,1)} async-done(((bf16[1,2,704,1408]{3,2,1,0:T(8,128)(2,1)}), bf16[1,2,352,1408]{3,2,1,0:T(8,128)(2,1)}) %reduce-scatter.4.cloned.1.call-update) | async-done | bytes 1982480 | tf_op jit(solution)/shard_map/reduce_scatter | solution.py:123
  413.8 58.6 %reduce-scatter.6.cloned.1.call-done = bf16[1,1408,768]{2,1,0:T(8,128)(2,1)} async-done(((bf16[1,1408,1536]{2,1,0:T(8,128)(2,1)}), bf16[1,1408,768]{2,1,0:T(8,128)(2,1)}) %reduce-scatter.6.cloned.1.call-update) | async-done | bytes 2162704 | tf_op jit(solution)/shard_map/reduce_scatter | solution.py:126
  472.4 58.7 %reduce-scatter.8.cloned.1.call-done = bf16[1,768,1408]{2,1,0:T(8,128)(2,1)} async-done(((bf16[1,1536,1408]{2,1,0:T(8,128)(2,1)}), bf16[1,768,1408]{2,1,0:T(8,128)(2,1)}) %reduce-scatter.8.cloned.1.call-update) | async-done | bytes 2162704 | tf_op jit(solution)/shard_map/reduce_scatter | solution.py:129
  (179 shorter events, 58.9 us)
Async XLA Ops:
  7.2 63.3 %all-gather.7.cloned.1.call-start = ((), (), s32[]{:S(2)}) async-start(), calls=%async_computation.4 | async-start | bytes 6488064 | tf_op jit(solution)/shard_map/all_gather | solution.py:52
  7.9 122.3 %all-gather.5.cloned.1.call-start = ((), (), s32[]{:S(2)}) async-start(), calls=%async_computation.3 | async-start | bytes 6488064 | tf_op jit(solution)/shard_map/all_gather | solution.py:53
  8.7 177.3 %all-gather.11.cloned.1.call-start = ((), (), s32[]{:S(2)}) async-start(), calls=%async_computation.6 | async-start | bytes 5947392 | tf_op jit(solution)/shard_map/all_gather | solution.py:51
  9.4 199.6 %all-gather.9.cloned.1.call-start = ((), (), s32[]{:S(2)}) async-start(), calls=%async_computation.5 | async-start | bytes 1622016 | tf_op jit(solution)/shard_map/all_gather | solution.py:60
  10.4 64.1 %copy-start.25 = (bf16[128,1408]{1,0:T(8,128)(2,1)}, bf16[128,1408]{1,0:T(8,128)(2,1)S(1)}, u32[]{:S(2)}) copy-start(bf16[128,1408]{1,0:T(8,128)(2,1)S(1)} %gather_fusion.4) | copy-start | bytes 1081348
  70.5 63.8 %slice-start = ((s8[4325376]{0:T(1024)(128)(4,1)}), s8[131072]{0:T(1024)(128)(4,1)S(1)}, s32[]{:S(2)}) async-start(s8[4325376]{0:T(1024)(128)(4,1)} %bitcast.149), calls=%async_computation.10 | async-start | bytes 262144
  135.8 17.8 %collective-permute-start = (f32[128,1408]{1,0:T(8,128)S(1)}, f32[128,1408]{1,0:T(8,128)S(1)}, u32[]{:S(2)}, u32[]{:S(2)}) collective-permute-start(f32[128,1408]{1,0:T(8,128)S(1)} %fusion.14), channel_id=1, source_target_pairs={{0,2},{2,0},{1,3},{3,1},{4,6},{6,4},{5,7},{7,5},{8,10},{10,8},{9,1... | collective-permute-start | bytes 2162696 | tf_op jit(solution)/shard_map/ppermute | solution.py:12
  137.4 276.4 %reduce-scatter.4.cloned.1.call-start = ((), (), s32[]{:S(2)}) async-start(), calls=%async_computation.7 | async-start | bytes 5947392 | tf_op jit(solution)/shard_map/reduce_scatter | solution.py:123
  153.7 36.7 %copy-start.4 = (bf16[128,1408]{1,0:T(8,128)(2,1)}, bf16[128,1408]{1,0:T(8,128)(2,1)S(1)}, u32[]{:S(2)}) copy-start(bf16[128,1408]{1,0:T(8,128)(2,1)S(1)} %add_convert_fusion.3) | copy-start | bytes 1081348
  189.4 1.5 collective-permute-start.2
  190.4 28.8 %copy-start.27 = (bf16[128,1408]{1,0:T(8,128)(2,1)}, bf16[128,1408]{1,0:T(8,128)(2,1)S(1)}, u32[]{:S(2)}) copy-start(bf16[128,1408]{1,0:T(8,128)(2,1)S(1)} %gather_fusion.5) | copy-start | bytes 1081348
  190.8 21.0 %collective-permute-start.3 = (bf16[128,704]{0,1:T(8,128)(2,1)S(1)}, bf16[128,704]{0,1:T(8,128)(2,1)S(1)}, u32[]{:S(2)}, u32[]{:S(2)}) collective-permute-start(bf16[128,704]{0,1:T(8,128)(2,1)S(1)} %collective-permute-done.2), channel_id=1, source_target_pairs={{0,8},{4,12},{8,0},{12,4},{16,24},{20,28},{24,16},{28,20},{1,9},{5... | collective-permute-start | bytes 540680 | tf_op jit(solution)/shard_map/ppermute | solution.py:22
  210.6 8.6 %collective-permute-start.1 = (bf16[128,704]{0,1:T(8,128)(2,1)S(1)}, bf16[128,704]{0,1:T(8,128)(2,1)S(1)}, u32[]{:S(2)}, u32[]{:S(2)}) collective-permute-start(bf16[128,704]{0,1:T(8,128)(2,1)S(1)} %get-tuple-element.11), channel_id=1, source_target_pairs={{4,0},{8,4},{12,8},{16,12},{20,16},{24,20},{28,24},{5,1},{9,5},{13... | collective-permute-start | bytes 540680 | tf_op jit(solution)/shard_map/ppermute | solution.py:28
  211.9 14.2 %collective-permute-start.4 = (bf16[128,704]{0,1:T(8,128)(2,1)S(1)}, bf16[128,704]{0,1:T(8,128)(2,1)S(1)}, u32[]{:S(2)}, u32[]{:S(2)}) collective-permute-start(bf16[128,704]{0,1:T(8,128)(2,1)S(1)} %collective-permute-done.3), channel_id=1, source_target_pairs={{0,16},{4,20},{8,24},{12,28},{16,0},{20,4},{24,8},{28,12},{1,17},{... | collective-permute-start | bytes 540680 | tf_op jit(solution)/shard_map/ppermute | solution.py:22
  232.6 21.1 %copy-start.6 = (bf16[128,1408]{1,0:T(8,128)(2,1)}, bf16[128,1408]{1,0:T(8,128)(2,1)S(1)}, u32[]{:S(2)}) copy-start(bf16[128,1408]{1,0:T(8,128)(2,1)S(1)} %bitcast_select_fusion.2) | copy-start | bytes 1081348
  236.8 17.0 %copy-start.2 = (bf16[1,2,704,1408]{3,2,1,0:T(8,128)(2,1)S(1)}, bf16[1,2,704,1408]{3,2,1,0:T(8,128)(2,1)}, u32[]{:S(2)}) copy-start(bf16[1,2,704,1408]{3,2,1,0:T(8,128)(2,1)} %all-gather.11.cloned.1.call-done) | copy-start | bytes 11894788
  238.4 15.3 %collective-permute-start.5 = (f32[128,1408]{1,0:T(8,128)S(1)}, f32[128,1408]{1,0:T(8,128)S(1)}, u32[]{:S(2)}, u32[]{:S(2)}) collective-permute-start(f32[128,1408]{1,0:T(8,128)S(1)} %fusion.10), channel_id=1, source_target_pairs={{0,2},{2,0},{1,3},{3,1},{4,6},{6,4},{5,7},{7,5},{8,10},{10,8},{9,1... | collective-permute-start | bytes 2162696 | tf_op jit(solution)/shard_map/ppermute | solution.py:12
  255.1 1.5 collective-permute-start.7
  256.5 6.6 %collective-permute-start.8 = (bf16[128,704]{0,1:T(8,128)(2,1)S(1)}, bf16[128,704]{0,1:T(8,128)(2,1)S(1)}, u32[]{:S(2)}, u32[]{:S(2)}) collective-permute-start(bf16[128,704]{0,1:T(8,128)(2,1)S(1)} %collective-permute-done.7), channel_id=1, source_target_pairs={{0,8},{4,12},{8,0},{12,4},{16,24},{20,28},{24,16},{28,20},{1,9},{5... | collective-permute-start | bytes 540680 | tf_op jit(solution)/shard_map/ppermute | solution.py:22
  259.4 11.3 %collective-permute-start.6 = (bf16[128,704]{0,1:T(8,128)(2,1)S(1)}, bf16[128,704]{0,1:T(8,128)(2,1)S(1)}, u32[]{:S(2)}, u32[]{:S(2)}) collective-permute-start(bf16[128,704]{0,1:T(8,128)(2,1)S(1)} %get-tuple-element.9), channel_id=1, source_target_pairs={{4,0},{8,4},{12,8},{16,12},{20,16},{24,20},{28,24},{5,1},{9,5},{13... | collective-permute-start | bytes 540680 | tf_op jit(solution)/shard_map/ppermute | solution.py:28
  263.1 12.8 %collective-permute-start.9 = (bf16[128,704]{0,1:T(8,128)(2,1)S(1)}, bf16[128,704]{0,1:T(8,128)(2,1)S(1)}, u32[]{:S(2)}, u32[]{:S(2)}) collective-permute-start(bf16[128,704]{0,1:T(8,128)(2,1)S(1)} %collective-permute-done.8), channel_id=1, source_target_pairs={{0,16},{4,20},{8,24},{12,28},{16,0},{20,4},{24,8},{28,12},{1,17},{... | collective-permute-start | bytes 540680 | tf_op jit(solution)/shard_map/ppermute | solution.py:22
  282.6 21.6 %copy-start.10 = (bf16[128,1408]{1,0:T(8,128)(2,1)}, bf16[128,1408]{1,0:T(8,128)(2,1)S(1)}, u32[]{:S(2)}) copy-start(bf16[128,1408]{1,0:T(8,128)(2,1)S(1)} %bitcast_select_fusion.1) | copy-start | bytes 1081348
  286.9 17.5 %copy-start.3 = (bf16[1,2,704,1408]{3,2,1,0:T(8,128)(2,1)S(1)}, bf16[1,2,704,1408]{3,2,1,0:T(8,128)(2,1)}, u32[]{:S(2)}) copy-start(bf16[1,2,704,1408]{3,2,1,0:T(8,128)(2,1)} %all-gather.11.cloned.1.call-done) | copy-start | bytes 11894788
  288.4 15.8 %collective-permute-start.10 = (f32[128,1408]{1,0:T(8,128)S(1)}, f32[128,1408]{1,0:T(8,128)S(1)}, u32[]{:S(2)}, u32[]{:S(2)}) collective-permute-start(f32[128,1408]{1,0:T(8,128)S(1)} %fusion.6), channel_id=1, source_target_pairs={{0,2},{2,0},{1,3},{3,1},{4,6},{6,4},{5,7},{7,5},{8,10},{10,8},{9,1... | collective-permute-start | bytes 2162696 | tf_op jit(solution)/shard_map/ppermute | solution.py:12
  305.6 1.5 collective-permute-start.12
  307.1 6.8 %collective-permute-start.13 = (bf16[128,704]{0,1:T(8,128)(2,1)S(1)}, bf16[128,704]{0,1:T(8,128)(2,1)S(1)}, u32[]{:S(2)}, u32[]{:S(2)}) collective-permute-start(bf16[128,704]{0,1:T(8,128)(2,1)S(1)} %collective-permute-done.12), channel_id=1, source_target_pairs={{0,8},{4,12},{8,0},{12,4},{16,24},{20,28},{24,16},{28,20},{1,9},{5... | collective-permute-start | bytes 540680 | tf_op jit(solution)/shard_map/ppermute | solution.py:22
  310.2 11.0 %collective-permute-start.11 = (bf16[128,704]{0,1:T(8,128)(2,1)S(1)}, bf16[128,704]{0,1:T(8,128)(2,1)S(1)}, u32[]{:S(2)}, u32[]{:S(2)}) collective-permute-start(bf16[128,704]{0,1:T(8,128)(2,1)S(1)} %get-tuple-element.7), channel_id=1, source_target_pairs={{4,0},{8,4},{12,8},{16,12},{20,16},{24,20},{28,24},{5,1},{9,5},{13... | collective-permute-start | bytes 540680 | tf_op jit(solution)/shard_map/ppermute | solution.py:28
  313.9 12.8 %collective-permute-start.14 = (bf16[128,704]{0,1:T(8,128)(2,1)S(1)}, bf16[128,704]{0,1:T(8,128)(2,1)S(1)}, u32[]{:S(2)}, u32[]{:S(2)}) collective-permute-start(bf16[128,704]{0,1:T(8,128)(2,1)S(1)} %collective-permute-done.13), channel_id=1, source_target_pairs={{0,16},{4,20},{8,24},{12,28},{16,0},{20,4},{24,8},{28,12},{1,17},{... | collective-permute-start | bytes 540680 | tf_op jit(solution)/shard_map/ppermute | solution.py:22
  338.7 15.9 %collective-permute-start.15 = (f32[128,1408]{1,0:T(8,128)S(1)}, f32[128,1408]{1,0:T(8,128)}, u32[]{:S(2)}, u32[]{:S(2)}) collective-permute-start(f32[128,1408]{1,0:T(8,128)S(1)} %fusion.2), channel_id=1, source_target_pairs={{0,2},{2,0},{1,3},{3,1},{4,6},{6,4},{5,7},{7,5},{8,10},{10,8},{9,1... | collective-permute-start | bytes 2162696 | tf_op jit(solution)/shard_map/ppermute | solution.py:12
  360.3 112.0 %reduce-scatter.6.cloned.1.call-start = ((), (), s32[]{:S(2)}) async-start(), calls=%async_computation.8 | async-start | bytes 6488064 | tf_op jit(solution)/shard_map/reduce_scatter | solution.py:126
  367.4 163.7 %reduce-scatter.8.cloned.1.call-start = ((), (), s32[]{:S(2)}) async-start(), calls=%async_computation.9 | async-start | bytes 6488064 | tf_op jit(solution)/shard_map/reduce_scatter | solution.py:129
  374.1 157.0 %copy-start.1 = (bf16[1,128,1408]{2,1,0:T(8,128)(2,1)S(1)}, bf16[1,128,1408]{2,1,0:T(8,128)(2,1)}, u32[]{:S(2)}) copy-start(bf16[1,128,1408]{2,1,0:T(8,128)(2,1)} %param.9) | copy-start | bytes 1081348
  (36 other events, 134.2 us)
Sparse Core Ops, SparseCore 0:
  9.5 60.9 all-gather.6
  72.0 58.1 all-gather.4
  131.8 54.1 all-gather.10
  187.4 21.6 all-gather.8
  360.5 53.2 reduce-scatter.3
  416.5 55.8 reduce-scatter.5
  475.3 55.7 reduce-scatter.7
